TPU v7x, 32 devices: a whole 2x2x4 slice. The times are simulated.
32 devices in a mesh: fsdp: 8 (over y, x, core), group: 4 (over z).
Axes of the slice: x: 2, y: 2, z: 4, core: 2. Of those that a mesh axis runs over, the one named last changes fastest.
Arguments:
- gradient: bfloat16 [4, 512, 4096], P('group', 'fsdp'), may hold values from -4000 to 4000
- first_moment: bfloat16 [4, 4096, 512], P('group', 'fsdp'), may hold values from -3 to 3
- second_moment: bfloat16 [4, 4096, 512], P('group', 'fsdp'), may hold values from 0.29882812 to 3
- basis_store: bfloat16 [4, 4608, 256], P('group', 'fsdp'), may hold values from -1 to 2
- step_number: int32 [1], replicated, may hold values from 1 to 99999
- matrix_ids: int32 [4], P('group'), may hold values from 0 to 3, each once
Outputs:
- update: bfloat16 [4, 512, 4096], P('group', 'fsdp')
- new_first: bfloat16 [4, 4096, 512], P('group', 'fsdp')
- new_second: bfloat16 [4, 4096, 512], P('group', 'fsdp')
Inputs may be any that keep to these rules, and one draw needn't show every extreme that they name: `matrix_ids`: each matrix index once.
All inputs are finite; a program needn't handle non-finite values.
Results may differ from a plain program's by a relative error of at most 0.0004.
Values may be sent and summed in bfloat16 or wider, within the bound.
A program may use at most 64 MiB of HBM per device.

v0:
```python
import math
import jax
import jax.numpy as jnp
from jax import lax
from jax.sharding import PartitionSpec as P

BLOCK = 256
BETA_ONE = 0.95
BETA_TWO = 0.95
ADAM_EPS = 1e-08
HIGHEST = lax.Precision.HIGHEST


def clip_of(local_squares, entries):
    total = lax.psum(local_squares, ("fsdp", "group"))
    return jnp.float32(math.sqrt(entries)) / (jnp.sqrt(total) + 1e-06)


def local(gradient, first_moment, second_moment, basis_store, step_number, matrix_ids):
    fsdp_count = lax.axis_size("fsdp")
    group_count = lax.axis_size("group")
    row_count = gradient.shape[1]
    col_count = gradient.shape[2]
    all_rows = row_count * fsdp_count
    col_share = col_count // fsdp_count
    left_blocks = all_rows // BLOCK
    right_blocks = col_count // BLOCK
    entries = all_rows * col_count * group_count
    grad_local = gradient[0].astype(jnp.float32)
    local_squares = jnp.sum(grad_local * grad_local)
    gathered = lax.all_gather(basis_store[0], "fsdp", axis=0, tiled=True)
    owner_rows = basis_store.shape[1]
    owner = (step_number[0] + matrix_ids[0]) % fsdp_count
    ordered_half = jnp.roll(gathered, -owner * owner_rows, axis=0)
    left = ordered_half[:all_rows].astype(jnp.float32).reshape(left_blocks, BLOCK, BLOCK)
    right_half = ordered_half[all_rows:].reshape(right_blocks, BLOCK, BLOCK)
    right = right_half.astype(jnp.float32)
    turned = jnp.einsum(
        "rbj,bjl->rbl",
        gradient[0].reshape(row_count, right_blocks, BLOCK),
        right_half,
        preferred_element_type=jnp.float32,
    )
    turned = clip_of(local_squares, entries) * turned
    outgoing = turned.reshape(row_count, fsdp_count, col_share)
    received = lax.all_to_all(outgoing, "fsdp", split_axis=1, concat_axis=0, tiled=True)
    width = received.shape[2]
    columns = received[:, 0, :].reshape(left_blocks, BLOCK, width)
    rotated = jnp.einsum("bkc,bki->cbi", columns, left, precision=HIGHEST).reshape(width, all_rows)
    count = step_number[0].astype(jnp.float32)
    first_fix = 1.0 - jnp.power(jnp.float32(BETA_ONE), count)
    second_fix = 1.0 - jnp.power(jnp.float32(BETA_TWO), count)
    first_sum = BETA_ONE * first_moment[0].astype(jnp.float32) + (1.0 - BETA_ONE) * rotated
    second_sum = (
        BETA_TWO * second_moment[0].astype(jnp.float32) + (1.0 - BETA_TWO) * rotated * rotated
    )
    direction = first_sum / first_fix / (jnp.sqrt(second_sum / second_fix) + ADAM_EPS)
    backward = jnp.einsum(
        "cbi,bki->cbk", direction.reshape(col_share, left_blocks, BLOCK), left, precision=HIGHEST
    )
    returning = backward.reshape(col_share, fsdp_count, row_count)
    received = lax.all_to_all(returning, "fsdp", split_axis=1, concat_axis=0, tiled=True)
    width = received.shape[2]
    pieces = received[:, 0, :].reshape(right_blocks, BLOCK, width)
    result = jnp.einsum("blr,bjl->rbj", pieces, right, precision=HIGHEST).reshape(width, col_count)
    return (
        result[None].astype(jnp.bfloat16),
        first_sum[None].astype(jnp.bfloat16),
        second_sum[None].astype(jnp.bfloat16),
    )


def solution(mesh):
    in_specs = (
        P("group", "fsdp", None),
        P("group", "fsdp", None),
        P("group", "fsdp", None),
        P("group", "fsdp", None),
        P(),
        P("group"),
    )
    out_specs = (P("group", "fsdp", None), P("group", "fsdp", None), P("group", "fsdp", None))
    return jax.shard_map(local, mesh=mesh, in_specs=in_specs, out_specs=out_specs, check_vma=False)
```

profile of v0, /device:TPU:0, one launch (start us, length us, event | category | flops | bytes accessed | tf_op | source)
XLA Modules:
  0.0 129.9 jit_solution(4664834779437250794)
XLA Ops:
  7.2 0.0 all-gather.3.cloned.1.call-start
  7.2 0.7 all-gather.3.cloned.1.call-update
  7.9 1.9 %multiply_reduce_fusion = f32[]{:T(128)} fusion(bf16[1,64,4096]{2,1,0:T(8,128)(2,1)} %param.6), kind=kLoop, calls=%fused_computation.24 | loop fusion | flops 786431 | bytes 524292 | tf_op jit(solution)/shard_map/reduce_sum | solution.py:30
  9.8 42.2 %psum.7 = f32[]{:T(128)} all-reduce(f32[]{:T(128)} %multiply_reduce_fusion), channel_id=1, replica_groups=mesh['fsdp'=8,'group'=4] {'fsdp','group'}, use_global_device_ids=true, to_apply=%region_1.2 | all-reduce | flops 1 | bytes 8 | tf_op jit(solution)/shard_map/psum | solution.py:15
  54.0 1.1 copy.42
  55.2 0.0 all-gather.3.cloned.1.call-done
  55.3 3.7 %fusion = bf16[4608,256]{1,0:T(8,128)(2,1)S(1)} fusion(s32[]{:T(128)S(6)} %select_n.21, bf16[4608,256]{1,0:T(8,128)(2,1)} %bitcast.46), kind=kLoop, calls=%fused_computation.2 | loop fusion | flops 4718592 | bytes 4718596 | tf_op jit(solution)/shard_map/jit(_roll_dynamic)/concatenate | solution.py:34
  59.0 0.0 copy-start
  59.0 0.1 slice.8
  59.2 0.5 fusion.1
  59.6 0.8 copy-done
  60.4 0.6 copy.30
  61.0 1.3 %reshape.80 = f32[64,8,512]{2,1,0:T(8,128)} reshape(f32[64,16,256]{2,1,0:T(8,128)S(1)} %copy.30) | data formatting | bytes 2097152 | tf_op jit(solution)/shard_map/reshape | solution.py:45
  62.3 2.8 %copy.31 = f32[64,8,512]{2,0,1:T(8,128)} copy(f32[64,8,512]{2,1,0:T(8,128)} %reshape.80) | data formatting | bytes 2097152 | tf_op jit(solution)/shard_map/reshape | solution.py:45
  65.1 3.8 %all-to-all-start = ((f32[64,8,512]{2,0,1:T(8,128)}), f32[64,8,512]{2,0,1:T(8,128)S(1)}, u32[]{:S(2)}, u32[]{:S(2)}) async-start(f32[64,8,512]{2,0,1:T(8,128)} %copy.31), calls=%async_computation | async-start | bytes 2097152 | tf_op jit(solution)/shard_map/all_to_all | solution.py:46
  69.0 1.0 slice.9
  69.9 14.4 %all-to-all-done = f32[64,8,512]{2,0,1:T(8,128)S(1)} async-done(((f32[64,8,512]{2,0,1:T(8,128)}), f32[64,8,512]{2,0,1:T(8,128)S(1)}, u32[]{:S(2)}, u32[]{:S(2)}) %all-to-all-start) | async-done | bytes 1048608 | tf_op jit(solution)/shard_map/all_to_all | solution.py:46
  84.3 1.7 %fusion.23 = f32[2,256,512]{2,1,0:T(8,128)} fusion(bf16[2,256,256]{2,1,0:T(8,128)(2,1)S(1)} %bitcast.49, f32[2,256,512]{2,1,0:T(8,128)S(1)} %bitcast.43), kind=kOutput, calls=%fused_computation.32 | convolution fusion | flops 805306368 | bytes 2359296 | tf_op jit(solution)/shard_map/bkc,bki->cbi/dot_general | solution.py:49
  86.0 2.5 %copy.38 = f32[1,512,512]{2,1,0:T(8,128)} copy(f32[1,512,512]{1,2,0:T(8,128)} %bitcast.44) | data formatting | bytes 2097152 | tf_op jit(solution)/shard_map/reshape | solution.py:49
  88.6 3.0 %fusion.14 = (bf16[1,512,512]{2,1,0:T(8,128)(2,1)}, bf16[1,512,512]{2,1,0:T(8,128)(2,1)}, f32[1,512,512]{2,1,0:T(8,128)}, f32[1,512,512]{2,1,0:T(8,128)S(1)}) fusion(f32[1,512,512]{2,1,0:T(8,128)} %copy.38, bf16[1,512,512]{2,1,0:T(8,128)(2,1)} %param.8, bf16[1,512,512]{2,1,0:T(8,128)(2,1)} %param.7), kind=kLoop, calls=%fused_computation.20 | loop fusion | flops 2621440 | bytes 5242880 | tf_op jit(solution)/shard_map/convert_element_type | solution.py:69
  91.6 2.6 %copy.28 = f32[1,512,512]{1,2,0:T(8,128)} copy(f32[1,512,512]{2,1,0:T(8,128)} %get-tuple-element.5) | data formatting | bytes 2097152 | tf_op jit(solution)/shard_map/mul | solution.py:53
  94.2 1.3 %copy.33 = f32[1,512,512]{1,2,0:T(8,128)} copy(f32[1,512,512]{2,1,0:T(8,128)S(1)} %get-tuple-element.6) | data formatting | bytes 2097152 | tf_op jit(solution)/shard_map/mul | solution.py:55
  95.5 3.1 %fusion.4 = f32[2,256,512]{2,1,0:T(8,128)S(1)} fusion(bf16[2,256,256]{2,1,0:T(8,128)(2,1)S(1)} %bitcast.50, f32[512,2,256]{0,2,1:T(8,128)} %bitcast.51, f32[512,2,256]{0,2,1:T(8,128)} %bitcast.52, f32[2,256,512]{2,1,0:T(8,128)} %fusion.23, f32[]{:T(128)} %bitcast.10), kind=kOutput, calls=%fused_computation.12 | convolution fusion | flops 807403520 | bytes 4456452 | tf_op jit(solution)/shard_map/cbi,bki->cbk/dot_general | solution.py:58
  98.6 17.8 %all_to_all.30 = f32[512,8,64]{0,2,1:T(8,128)S(1)} all-to-all(f32[512,8,64]{0,2,1:T(8,128)S(1)} %bitcast.53), channel_id=1, replica_groups=mesh['fsdp'=8,'group'=4] {'fsdp'}, dimensions={1} | all-to-all | bytes 2097152 | tf_op jit(solution)/shard_map/all_to_all | solution.py:62
  116.4 1.6 %copy.35 = f32[8,512,1,64]{1,0,3,2:T(8,128)} copy(f32[8,512,1,64]{1,3,0,2:T(8,128)S(1)} %bitcast.45) | data formatting | bytes 2097152 | tf_op jit(solution)/shard_map/all_to_all | solution.py:62
  118.0 1.4 %reshape_squeeze.11 = f32[16,256,64]{1,0,2:T(8,128)S(1)} reshape(f32[8,512,1,64]{1,0,3,2:T(8,128)} %copy.35) | data formatting | bytes 2097152 | tf_op jit(solution)/shard_map/reshape;squeeze | solution.py:64
  119.4 2.3 %fusion.2 = bf16[64,16,256]{2,0,1:T(8,128)(2,1)S(1)} fusion(bf16[16,256,256]{2,1,0:T(8,128)(2,1)S(1)} %bitcast.42, f32[16,256,64]{1,0,2:T(8,128)S(1)} %reshape_squeeze.11), kind=kOutput, calls=%fused_computation.10 | convolution fusion | flops 805568512 | bytes 3670016 | tf_op jit(solution)/shard_map/blr,bjl->rbj/dot_general | solution.py:65
  121.7 0.3 copy.37
  122.0 1.0 convert_element_type.55
Async XLA Ops:
  7.2 48.1 %all-gather.3.cloned.1.call-start = ((), (), s32[]{:S(2)}) async-start(), calls=%async_computation.2 | async-start | bytes 2654208 | tf_op jit(solution)/shard_map/all_gather | solution.py:31
  59.0 1.4 %copy-start = (bf16[4608,256]{1,0:T(8,128)(2,1)}, bf16[4608,256]{1,0:T(8,128)(2,1)S(1)}, u32[]{:S(2)}) copy-start(bf16[4608,256]{1,0:T(8,128)(2,1)S(1)} %fusion) | copy-start | bytes 7077892
  65.1 19.2 %all-to-all-start = ((f32[64,8,512]{2,0,1:T(8,128)}), f32[64,8,512]{2,0,1:T(8,128)S(1)}, u32[]{:S(2)}, u32[]{:S(2)}) async-start(f32[64,8,512]{2,0,1:T(8,128)} %copy.31), calls=%async_computation | async-start | bytes 2097152 | tf_op jit(solution)/shard_map/all_to_all | solution.py:46
Sparse Core Ops, SparseCore 0:
  9.9 31.9 all-gather.2
where the time goes:
time: 131 us; the launch traced here: 130 us
  blocking collectives  60 us (46%)
  local copies, waits for them, and re-layouts  18.5 us (14%)
  between operations  16.2 us (12%)
  waiting for transfers between devices  15.1 us (12%)
  other arithmetic  8.67 us (7%)
  matrix products  7.53 us (6%)
  starting transfers between devices  3.82 us (3%)
    psum x1, blocking collectives, clip_of(): total = lax.psum(local_squares, ('fsdp', 'group'))  42.2 us
    all_to_all x1, blocking collectives, local(): lax.all_to_all(returning, 'fsdp', split_axis=1, concat_axis=0, tiled=True)  17.8 us
    all_to_all x1, waiting for transfers between devices, local(): lax.all_to_all(outgoing, 'fsdp', split_axis=1, concat_axis=0, tiled=True)  14.4 us
    reshape x2, local copies, waits for them, and re-layouts, local(): outgoing = turned.reshape(row_count, fsdp_count, col_share)  4.1 us
    all_to_all x1, starting transfers between devices, local(): lax.all_to_all(outgoing, 'fsdp', split_axis=1, concat_axis=0, tiled=True)  3.79 us
    concatenate x1, other arithmetic, local(): ordered_half = jnp.roll(gathered, -owner * owner_rows, axis=0)  3.73 us
    dot_general x1, matrix products, local(): jnp.einsum('cbi,bki->cbk', direction.reshape(col_share, left_blocks, BLOC...  3.12 us
    convert_element_type x1, other arithmetic, local(): second_sum[None].astype(jnp.bfloat16)  3.02 us
  transfers between devices with their start and end apart: 2, of which 1 were waited for; matrix products, arithmetic and copies ran while one was open for 3% of the time, Pallas kernels for 0%

commit v1 on v0

--- a/solution.py
+++ b/solution.py
@@ -9,6 +9,29 @@
 BETA_TWO = 0.95
 ADAM_EPS = 1e-08
 HIGHEST = lax.Precision.HIGHEST
+
+
+def split_up(array, dim, peers):
+    lengths = array.shape
+    pieces = array.reshape(*lengths[:dim], peers, lengths[dim] // peers, *lengths[dim + 1 :])
+    return jnp.moveaxis(pieces, dim, 0)
+
+
+def joined_along(parts, dim):
+    parts = jnp.moveaxis(parts, 0, dim)
+    shape = parts.shape
+    return parts.reshape(*shape[:dim], shape[dim] * shape[dim + 1], *shape[dim + 2 :])
+
+
+def swapped_with_each(shard, axis, split_dim, concat_dim):
+    size, position = (lax.axis_size(axis), lax.axis_index(axis))
+    parts = split_up(shard, split_dim, size)
+    finished = [parts[position]]
+    for turn in range(1, size):
+        sent = parts[position ^ turn]
+        finished.append(lax.ppermute(sent, axis, [(i, i ^ turn) for i in range(size)]))
+    parts = jnp.stack(finished)[position ^ jnp.arange(size)]
+    return joined_along(parts, concat_dim)
 
 
 def clip_of(local_squares, entries):
@@ -59,7 +82,7 @@
         "cbi,bki->cbk", direction.reshape(col_share, left_blocks, BLOCK), left, precision=HIGHEST
     )
     returning = backward.reshape(col_share, fsdp_count, row_count)
-    received = lax.all_to_all(returning, "fsdp", split_axis=1, concat_axis=0, tiled=True)
+    received = swapped_with_each(returning, "fsdp", 1, 0)
     width = received.shape[2]
     pieces = received[:, 0, :].reshape(right_blocks, BLOCK, width)
     result = jnp.einsum("blr,bjl->rbj", pieces, right, precision=HIGHEST).reshape(width, col_count)

time: 131 us -> 132 us (level)
  blocking collectives: 60 us -> 42.2 us
  waiting for transfers between devices: 15.1 us -> 24.8 us
  starting transfers between devices: 3.82 us -> 8.8 us
  local copies, waits for them, and re-layouts: 18.5 us -> 23.1 us
    all_to_all x1 -> x0, blocking collectives: 17.8 us -> none  [local(): lax.all_to_all(returning, 'fsdp', split_axis=1, concat_axis=0, tiled=True)]
    ppermute x0 -> x7, waiting for transfers between devices: none -> 9.72 us  [swapped_with_each(): lax.ppermute(sent, axis, [(i, i ^ turn) for i in range(size)])]
    ppermute x0 -> x7, starting transfers between devices: none -> 4.98 us  [swapped_with_each(): lax.ppermute(sent, axis, [(i, i ^ turn) for i in range(size)])]
    gather x0 -> x2, local copies, waits for them, and re-layouts: none -> 3.42 us  [swapped_with_each(): parts = jnp.stack(finished)[position ^ jnp.arange(size)]]
    unnamed x3 -> x12, local copies, waits for them, and re-layouts: 1.95 us -> 3.88 us
    all_to_all x1 -> x0, local copies, waits for them, and re-layouts: 1.59 us -> none  [local(): lax.all_to_all(returning, 'fsdp', split_axis=1, concat_axis=0, tiled=True)]
  transfers between devices with their start and end apart: 2 -> 9, of which waited for: 1 -> 4; matrix products, arithmetic and copies ran while one was open for 3% -> 4% of each run, Pallas kernels for 0% -> 0%
where the time goes in v1:
time: 132 us
  blocking collectives  42.2 us (32%)
  waiting for transfers between devices  24.8 us (19%)
  local copies, waits for them, and re-layouts  23.1 us (18%)
  between operations  16.3 us (12%)
  starting transfers between devices  8.8 us (7%)
  other arithmetic  8.78 us (7%)
  matrix products  7.53 us (6%)
    psum x1, blocking collectives, clip_of(): total = lax.psum(local_squares, ('fsdp', 'group'))  42.2 us
    all_to_all x1, waiting for transfers between devices, local(): lax.all_to_all(outgoing, 'fsdp', split_axis=1, concat_axis=0, tiled=True)  14.4 us
    ppermute x7, waiting for transfers between devices, swapped_with_each(): lax.ppermute(sent, axis, [(i, i ^ turn) for i in range(size)])  9.72 us
    ppermute x7, starting transfers between devices, swapped_with_each(): lax.ppermute(sent, axis, [(i, i ^ turn) for i in range(size)])  4.98 us
    reshape x2, local copies, waits for them, and re-layouts, local(): outgoing = turned.reshape(row_count, fsdp_count, col_share)  4.07 us
    unnamed x12, local copies, waits for them, and re-layouts  3.88 us
    all_to_all x1, starting transfers between devices, local(): lax.all_to_all(outgoing, 'fsdp', split_axis=1, concat_axis=0, tiled=True)  3.79 us
    concatenate x1, other arithmetic, local(): ordered_half = jnp.roll(gathered, -owner * owner_rows, axis=0)  3.73 us
  transfers between devices with their start and end apart: 9, of which 4 were waited for; matrix products, arithmetic and copies ran while one was open for 4% of the time, Pallas kernels for 0%

profile of v1, /device:TPU:0, one launch (start us, length us, event | category | flops | bytes accessed | tf_op | source)
XLA Modules:
  0.0 131.5 jit_solution(7482946896449429764)
XLA Ops:
  7.2 0.0 all-gather.3.cloned.1.call-start
  7.2 0.7 all-gather.3.cloned.1.call-update
  7.9 1.9 %multiply_reduce_fusion = f32[]{:T(128)} fusion(bf16[1,64,4096]{2,1,0:T(8,128)(2,1)} %param.6), kind=kLoop, calls=%fused_computation.25 | loop fusion | flops 786431 | bytes 524292 | tf_op jit(solution)/shard_map/reduce_sum | solution.py:53
  9.8 42.2 %psum.7 = f32[]{:T(128)} all-reduce(f32[]{:T(128)} %multiply_reduce_fusion), channel_id=1, replica_groups=mesh['fsdp'=8,'group'=4] {'fsdp','group'}, use_global_device_ids=true, to_apply=%region_1.2 | all-reduce | flops 1 | bytes 8 | tf_op jit(solution)/shard_map/psum | solution.py:38
  53.3 1.1 copy.53
  55.2 0.0 all-gather.3.cloned.1.call-done
  55.3 3.7 %fusion = bf16[4608,256]{1,0:T(8,128)(2,1)S(1)} fusion(s32[]{:T(128)S(6)} %select_n.55, bf16[4608,256]{1,0:T(8,128)(2,1)} %bitcast.74), kind=kLoop, calls=%fused_computation.3 | loop fusion | flops 4718592 | bytes 4718596 | tf_op jit(solution)/shard_map/jit(_roll_dynamic)/concatenate | solution.py:57
  59.0 0.0 copy-start
  59.0 0.1 slice.10
  59.1 0.5 fusion.1
  59.6 0.8 copy-done
  60.4 0.6 copy.41
  61.0 1.3 reshape.107
  62.3 2.8 %copy.42 = f32[64,8,512]{2,0,1:T(8,128)} copy(f32[64,8,512]{2,1,0:T(8,128)} %reshape.107) | data formatting | bytes 2097152 | tf_op jit(solution)/shard_map/reshape | solution.py:68
  65.1 3.8 %all-to-all-start = ((f32[64,8,512]{2,0,1:T(8,128)}), f32[64,8,512]{2,0,1:T(8,128)S(1)}, u32[]{:S(2)}, u32[]{:S(2)}) async-start(f32[64,8,512]{2,0,1:T(8,128)} %copy.42), calls=%async_computation | async-start | bytes 2097152 | tf_op jit(solution)/shard_map/all_to_all | solution.py:69
  68.9 1.0 slice.11
  69.9 14.4 %all-to-all-done = f32[64,8,512]{2,0,1:T(8,128)S(1)} async-done(((f32[64,8,512]{2,0,1:T(8,128)}), f32[64,8,512]{2,0,1:T(8,128)S(1)}, u32[]{:S(2)}, u32[]{:S(2)}) %all-to-all-start) | async-done | bytes 1048608 | tf_op jit(solution)/shard_map/all_to_all | solution.py:69
  84.3 1.7 %fusion.24 = f32[2,256,512]{2,1,0:T(8,128)} fusion(bf16[2,256,256]{2,1,0:T(8,128)(2,1)S(1)} %bitcast.79, f32[2,256,512]{2,1,0:T(8,128)S(1)} %bitcast.72), kind=kOutput, calls=%fused_computation.51 | convolution fusion | flops 805306368 | bytes 2359296 | tf_op jit(solution)/shard_map/bkc,bki->cbi/dot_general | solution.py:72
  85.9 2.5 %copy.49 = f32[1,512,512]{2,1,0:T(8,128)} copy(f32[1,512,512]{1,2,0:T(8,128)} %bitcast.73) | data formatting | bytes 2097152 | tf_op jit(solution)/shard_map/reshape | solution.py:72
  88.5 3.1 %fusion.14 = (bf16[1,512,512]{2,1,0:T(8,128)(2,1)}, bf16[1,512,512]{2,1,0:T(8,128)(2,1)}, f32[1,512,512]{2,1,0:T(8,128)S(1)}, f32[1,512,512]{2,1,0:T(8,128)}) fusion(f32[1,512,512]{2,1,0:T(8,128)} %copy.49, bf16[1,512,512]{2,1,0:T(8,128)(2,1)} %param.8, bf16[1,512,512]{2,1,0:T(8,128)(2,1)} %param.7), kind=kLoop, calls=%fused_computation.21 | loop fusion | flops 2621440 | bytes 5242880 | tf_op jit(solution)/shard_map/convert_element_type | solution.py:92
  91.6 2.6 %copy.44 = f32[1,512,512]{1,2,0:T(8,128)} copy(f32[1,512,512]{2,1,0:T(8,128)} %get-tuple-element.13) | data formatting | bytes 2097152 | tf_op jit(solution)/shard_map/mul | solution.py:78
  94.2 1.3 %copy.39 = f32[1,512,512]{1,2,0:T(8,128)} copy(f32[1,512,512]{2,1,0:T(8,128)S(1)} %get-tuple-element.12) | data formatting | bytes 2097152 | tf_op jit(solution)/shard_map/mul | solution.py:76
  95.5 3.1 %fusion.4 = f32[2,256,512]{2,1,0:T(8,128)S(1)} fusion(bf16[2,256,256]{2,1,0:T(8,128)(2,1)S(1)} %bitcast.80, f32[512,2,256]{0,2,1:T(8,128)} %bitcast.82, f32[512,2,256]{0,2,1:T(8,128)} %bitcast.81, f32[2,256,512]{2,1,0:T(8,128)} %fusion.24, f32[]{:T(128)} %bitcast.10), kind=kOutput, calls=%fused_computation.13 | convolution fusion | flops 807403520 | bytes 4456452 | tf_op jit(solution)/shard_map/cbi,bki->cbk/dot_general | solution.py:81
  98.6 0.8 dynamic-slice_bitcast_fusion
  99.5 0.0 collective-permute-start
  99.5 0.6 collective-permute-start.1
  100.1 1.3 collective-permute-start.2
  101.3 0.6 collective-permute-start.3
  101.9 1.1 collective-permute-start.4
  103.1 0.0 collective-permute-done
  103.1 0.7 collective-permute-start.5
  103.7 0.9 bitcast_dynamic-update-slice_fusion.6
  104.6 1.4 %collective-permute-done.1 = f32[512,1,64]{0,2,1:T(8,128)S(1)} collective-permute-done((f32[512,1,64]{0,2,1:T(8,128)}, f32[512,1,64]{0,2,1:T(8,128)S(1)}, u32[]{:S(2)}, u32[]{:S(2)}) %collective-permute-start.1) | collective-permute-done | bytes 131104 | tf_op jit(solution)/shard_map/ppermute | solution.py:32
  106.1 0.8 collective-permute-start.6
  106.8 1.1 collective-permute-done.2
  108.0 0.0 collective-permute-done.3
  108.0 7.2 %collective-permute-done.4 = f32[512,1,64]{0,2,1:T(8,128)S(1)} collective-permute-done((f32[512,1,64]{0,2,1:T(8,128)S(1)}, f32[512,1,64]{0,2,1:T(8,128)S(1)}, u32[]{:S(2)}, u32[]{:S(2)}) %collective-permute-start.4) | collective-permute-done | bytes 131104 | tf_op jit(solution)/shard_map/ppermute | solution.py:32
  115.2 0.0 collective-permute-done.5
  115.2 0.0 collective-permute-done.6
  115.2 0.0 copy-start.1
  115.2 1.0 copy-done.1
  116.2 1.8 %gather_fusion = f32[8,512,64]{1,2,0:T(8,128)S(1)} fusion(f32[8,512,64]{1,2,0:T(8,128)} %bitcast.71, s32[1024]{0:T(1024)S(1)} %pad_clamp_fusion), kind=kCustom, calls=%fused_computation | custom fusion | bytes 2097184 | tf_op jit(solution)/shard_map/gather | solution.py:33
  118.1 1.6 %copy.46 = f32[8,512,64]{1,0,2:T(8,128)} copy(f32[8,512,64]{1,2,0:T(8,128)S(1)} %gather_fusion) | data formatting | bytes 2097152 | tf_op jit(solution)/shard_map/gather | solution.py:33
  119.6 1.4 %reshape_squeeze_reshape.3 = f32[16,256,64]{1,0,2:T(8,128)S(1)} reshape(f32[8,512,64]{1,0,2:T(8,128)} %copy.46) | data formatting | bytes 2097152 | tf_op jit(solution)/shard_map/reshape;squeeze;reshape | solution.py:87
  121.1 2.3 %fusion.2 = bf16[64,16,256]{2,0,1:T(8,128)(2,1)S(1)} fusion(bf16[16,256,256]{2,1,0:T(8,128)(2,1)S(1)} %bitcast.70, f32[16,256,64]{1,0,2:T(8,128)S(1)} %reshape_squeeze_reshape.3), kind=kOutput, calls=%fused_computation.11 | convolution fusion | flops 805568512 | bytes 3670016 | tf_op jit(solution)/shard_map/blr,bjl->rbj/dot_general | solution.py:88
  123.3 0.3 copy.48
  123.6 1.0 convert_element_type.55
  (9 shorter events, 0.1 us)
Async XLA Ops:
  7.2 48.1 %all-gather.3.cloned.1.call-start = ((), (), s32[]{:S(2)}) async-start(), calls=%async_computation.1 | async-start | bytes 2654208 | tf_op jit(solution)/shard_map/all_gather | solution.py:54
  59.0 1.4 %copy-start = (bf16[4608,256]{1,0:T(8,128)(2,1)}, bf16[4608,256]{1,0:T(8,128)(2,1)S(1)}, u32[]{:S(2)}) copy-start(bf16[4608,256]{1,0:T(8,128)(2,1)S(1)} %fusion) | copy-start | bytes 7077892
  65.1 19.2 %all-to-all-start = ((f32[64,8,512]{2,0,1:T(8,128)}), f32[64,8,512]{2,0,1:T(8,128)S(1)}, u32[]{:S(2)}, u32[]{:S(2)}) async-start(f32[64,8,512]{2,0,1:T(8,128)} %copy.42), calls=%async_computation | async-start | bytes 2097152 | tf_op jit(solution)/shard_map/all_to_all | solution.py:69
  99.5 3.6 %collective-permute-start = (f32[512,1,64]{0,2,1:T(8,128)}, f32[512,1,64]{0,2,1:T(8,128)}, u32[]{:S(2)}, u32[]{:S(2)}) collective-permute-start(f32[512,1,64]{0,2,1:T(8,128)} %get-tuple-element.11), channel_id=1, source_target_pairs={{0,4},{4,0},{8,12},{12,8},{16,20},{20,16},{24,28},{28,24},{1,5},{5... | collective-permute-start | bytes 393224 | tf_op jit(solution)/shard_map/ppermute | solution.py:32
  99.5 6.6 %collective-permute-start.1 = (f32[512,1,64]{0,2,1:T(8,128)}, f32[512,1,64]{0,2,1:T(8,128)S(1)}, u32[]{:S(2)}, u32[]{:S(2)}) collective-permute-start(f32[512,1,64]{0,2,1:T(8,128)} %get-tuple-element.10), channel_id=1, source_target_pairs={{0,8},{4,12},{8,0},{12,4},{16,24},{20,28},{24,16},{28,20},{1,9},{5... | collective-permute-start | bytes 393224 | tf_op jit(solution)/shard_map/ppermute | solution.py:32
  100.1 7.9 %collective-permute-start.2 = (f32[512,1,64]{0,2,1:T(8,128)}, f32[512,1,64]{0,2,1:T(8,128)S(1)}, u32[]{:S(2)}, u32[]{:S(2)}) collective-permute-start(f32[512,1,64]{0,2,1:T(8,128)} %get-tuple-element.9), channel_id=1, source_target_pairs={{0,12},{4,8},{8,4},{12,0},{16,28},{20,24},{24,20},{28,16},{1,13},{... | collective-permute-start | bytes 393224 | tf_op jit(solution)/shard_map/ppermute | solution.py:32
  101.3 6.6 %collective-permute-start.3 = (f32[512,1,64]{0,2,1:T(8,128)}, f32[512,1,64]{0,2,1:T(8,128)S(1)}, u32[]{:S(2)}, u32[]{:S(2)}) collective-permute-start(f32[512,1,64]{0,2,1:T(8,128)} %get-tuple-element.8), channel_id=1, source_target_pairs={{0,16},{4,20},{8,24},{12,28},{16,0},{20,4},{24,8},{28,12},{1,17},{... | collective-permute-start | bytes 393224 | tf_op jit(solution)/shard_map/ppermute | solution.py:32
  101.9 13.3 %collective-permute-start.4 = (f32[512,1,64]{0,2,1:T(8,128)S(1)}, f32[512,1,64]{0,2,1:T(8,128)S(1)}, u32[]{:S(2)}, u32[]{:S(2)}) collective-permute-start(f32[512,1,64]{0,2,1:T(8,128)S(1)} %get-tuple-element.7), channel_id=1, source_target_pairs={{0,20},{4,16},{8,28},{12,24},{16,4},{20,0},{24,12},{28,8},{1,21},{... | collective-permute-start | bytes 393224 | tf_op jit(solution)/shard_map/ppermute | solution.py:32
  103.1 12.1 %collective-permute-start.5 = (f32[512,1,64]{0,2,1:T(8,128)S(1)}, f32[512,1,64]{0,2,1:T(8,128)S(1)}, u32[]{:S(2)}, u32[]{:S(2)}) collective-permute-start(f32[512,1,64]{0,2,1:T(8,128)S(1)} %get-tuple-element.6), channel_id=1, source_target_pairs={{0,24},{4,28},{8,16},{12,20},{16,8},{20,12},{24,0},{28,4},{1,25},{... | collective-permute-start | bytes 393224 | tf_op jit(solution)/shard_map/ppermute | solution.py:32
  106.1 9.1 %collective-permute-start.6 = (f32[512,1,64]{0,2,1:T(8,128)S(1)}, f32[512,1,64]{0,2,1:T(8,128)S(1)}, u32[]{:S(2)}, u32[]{:S(2)}) collective-permute-start(f32[512,1,64]{0,2,1:T(8,128)S(1)} %get-tuple-element.5), channel_id=1, source_target_pairs={{0,28},{4,24},{8,20},{12,16},{16,12},{20,8},{24,4},{28,0},{1,29},{... | collective-permute-start | bytes 393224 | tf_op jit(solution)/shard_map/ppermute | solution.py:32
  115.2 1.0 copy-start.1
Sparse Core Ops, SparseCore 0:
  9.9 31.9 all-gather.2
